TPU v7x, 32 devices: a whole 2x2x4 slice. The times are simulated.
32 devices in a mesh: gx: 8 (over z, x), gy: 4 (over y, core).
Axes of the slice: x: 2, y: 2, z: 4, core: 2. Of those that a mesh axis runs over, the one named last changes fastest.
Arguments:
- design: float32 [128, 256, 512], P('gx', 'gy'), may hold values from 0 to 1, as said below
- sensitivity: float32 [128, 256, 512], P('gx', 'gy'), may hold values from 0.1 to 10
- solid_mask: int32 [128, 256, 512], P('gx', 'gy'), may hold values 0 or 1
Outputs:
- new_design: float32 [128, 256, 512], P('gx', 'gy')
- objective_grad: float32 [128, 256, 512], P('gx', 'gy')
- multiplier: float32 [], replicated
Inputs may be any that keep to these rules, and one draw needn't show every extreme that they name: design densities lie strictly between 0 and 1.
All inputs are finite; a program needn't handle non-finite values. No bound on the sum of `solid_mask` on one device may be relied on, other than what follows from the above.
Results may differ from a plain program's by a relative error of at most 0.0003.
Values sent between devices are 32-bit elements; how exact they have to be, the bound alone decides.
A program may use at most 64 MiB of HBM per device.

v0:
```python
import functools
import math

import jax
import jax.numpy as jnp
from jax import lax
from jax.experimental import pallas as pl
from jax.experimental.pallas import tpu as pltpu
from jax.sharding import PartitionSpec as P

RADIUS = 8
DUAL_ITERS = 2
SPAN = RADIUS + 1
MESH = pl.DeviceIdType.MESH

beta_value = 4.0
eta_value = 0.5
volume_share = 0.4
move_limit = 0.2
asym_gap = 0.5
TANH_MID = math.tanh(beta_value * eta_value)
SCALE = math.tanh(beta_value * eta_value) + math.tanh(beta_value * (1.0 - eta_value))


def missing(distance):
    out = jnp.maximum(RADIUS - distance, 0)
    return (out * (out + 1)) // 2


def cover(cell, total):
    return (SPAN * SPAN - missing(cell) - missing(total - 1 - cell)).astype(jnp.float32)


def split2(x):
    hi = x.astype(jnp.bfloat16)
    lo = (x - hi.astype(jnp.float32)).astype(jnp.bfloat16)
    return hi, lo


def filter_zy(src, dst, group, first=0, rows=None):
    _, wide, depth = src.shape
    rows = src.shape[0] if rows is None else rows
    ry = wide - 2 * RADIUS
    jj = lax.broadcasted_iota(jnp.int32, (ry, wide), 0)
    bb = lax.broadcasted_iota(jnp.int32, (ry, wide), 1)
    band_y = jnp.maximum(SPAN - jnp.abs(jj + RADIUS - bb), 0).astype(jnp.float32).astype(jnp.bfloat16)
    cc = lax.broadcasted_iota(jnp.int32, (depth, depth), 0)
    kk = lax.broadcasted_iota(jnp.int32, (depth, depth), 1)
    band_z = jnp.maximum(SPAN - jnp.abs(cc - kk), 0).astype(jnp.float32).astype(jnp.bfloat16)

    def body(g, carry):
        his, los = [], []
        for r in range(group):
            hi, lo = split2(src[first + g * group + r])
            out = jnp.dot(band_y, hi, preferred_element_type=jnp.float32) + jnp.dot(
                band_y, lo, preferred_element_type=jnp.float32
            )
            hi, lo = split2(out)
            his.append(hi)
            los.append(lo)
        both = jnp.dot(
            jnp.concatenate(his + los, 0), band_z, preferred_element_type=jnp.float32
        )
        half = group * ry
        total = both[:half] + both[half:]
        for r in range(group):
            dst[first + g * group + r] = total[r * ry : (r + 1) * ry]
        return carry

    lax.fori_loop(0, rows // group, body, 0)


def filter_x(src, tile, emit):
    count = src.shape[0] - 2 * RADIUS
    load = lambda i: src[i, tile, :]
    box = load(0)
    for k in range(1, SPAN):
        box = box + load(k)
    window = [box]
    for n in range(1, SPAN):
        box = box + (load(n + RADIUS) - load(n - 1))
        window.append(box)
    total = window[0]
    for k in range(1, SPAN):
        total = total + window[k]
    emit(0, total)
    for i in range(1, count):
        n = i + RADIUS
        box = box + (load(n + RADIUS) - load(n - 1))
        total = total + (box - window[i - 1])
        window.append(box)
        emit(i, total)


(DES_UP, DES_DN, MASK, SENS, AFLD, A_UP, A_DN, V_UP, V_DN, O_UP, O_DN, VB,
 VY_UP, VY_DN, MASK_TWO, LAST) = range(16)
CHUNKS = 8
OB, OY_UP, OY_DN, COUNT = LAST, LAST + CHUNKS, LAST + 2 * CHUNKS, LAST + 3 * CHUNKS


def kernel(design, sens, mask, new_hbm, obj_hbm, lam_out, new_out, obj_out, vol_out, phys_out, full_mask, dbuf, afull, abuf, mbuf,
           sbuf, vbuf, obuf, vx, ox, vback, oback, ybox, xbox, send_sems, recv_sems, local_sems, y_send, y_recv,
           x_send, x_recv, obj_sems, new_sems):
    rows, ry, depth = design.shape
    half = depth // 2
    gx, gy = lax.axis_index("gx"), lax.axis_index("gy")
    nx, ny = lax.axis_size("gx"), lax.axis_size("gy")
    par = lax.rem(gx, 2)
    pair = gx // 2
    partner = gx + 1 - 2 * par
    has_xl, has_xr = gx >= 2, gx < nx - 2
    has_yl, has_yr = gy >= 1, gy < ny - 1
    xl, xr, yl, yr = (gx - 2, gy), (gx + 2, gy), (gx, gy - 1), (gx, gy + 1)
    mate = (partner, gy)

    barrier = pltpu.get_barrier_semaphore()

    def greet(dev):
        pl.semaphore_signal(barrier, inc=1, device_id=dev, device_id_type=MESH)

    for k in range(1, nx):
        greet((lax.rem(gx + k, nx), gy))
    for k in range(1, ny):
        greet((gx, lax.rem(gy + k, ny)))

    own = pl.ds(pl.multiple_of(par * half, 128), half)
    other = pl.ds(pl.multiple_of((1 - par) * half, 128), half)
    my_rows = pl.ds(par * rows, rows)
    mate_rows = pl.ds((1 - par) * rows, rows)
    mid = pl.ds(RADIUS, ry)

    l_des = pltpu.make_async_copy(design, dbuf.at[:, mid, :], local_sems.at[0])
    l_mask = pltpu.make_async_copy(mask.at[:, :, own], mbuf.at[my_rows], local_sems.at[1])
    l_sens = pltpu.make_async_copy(sens.at[:, :, own], sbuf.at[my_rows], local_sems.at[2])
    l_des.start()
    l_mask.start()
    l_sens.start()

    l_full = pltpu.make_async_copy(mask, full_mask, local_sems.at[6])
    l_full.start()
    pl.semaphore_wait(barrier, nx + ny - 2)

    def remote(idx, src, dst, dev):
        return pltpu.make_async_remote_copy(
            src_ref=src, dst_ref=dst, send_sem=send_sems.at[idx], recv_sem=recv_sems.at[idx],
            device_id=dev, device_id_type=MESH,
        )

    def y_pair(up, dn, src, off, buf):
        return (
            remote(up, src.at[:, pl.ds(off + ry - RADIUS, RADIUS), :], buf.at[:, pl.ds(0, RADIUS), :], yr),
            remote(dn, src.at[:, pl.ds(off, RADIUS), :], buf.at[:, pl.ds(RADIUS + ry, RADIUS), :], yl),
        )

    def x_pair(up, dn, buf):
        return (
            remote(up, buf.at[pl.ds(2 * rows, RADIUS)], buf.at[pl.ds(0, RADIUS)], xr),
            remote(dn, buf.at[pl.ds(RADIUS, RADIUS)], buf.at[pl.ds(RADIUS + 2 * rows, RADIUS)], xl),
        )

    def begin(two, low, high):
        pl.when(high)(lambda: two[0].start())
        pl.when(low)(lambda: two[1].start())

    def finish(two, low, high):
        pl.when(low)(lambda: two[0].wait_recv())
        pl.when(high)(lambda: two[1].wait_recv())

    def sent(two, low, high):
        pl.when(high)(lambda: two[0].wait_send())
        pl.when(low)(lambda: two[1].wait_send())

    r_des = y_pair(DES_UP, DES_DN, design, 0, dbuf)
    begin(r_des, has_yl, has_yr)
    ahead = max(rows // 2, 1)
    r_mask = remote(MASK, mask.at[pl.ds(0, ahead), :, other], mbuf.at[pl.ds(par * rows, ahead)], mate)
    r_mask.start()
    r_rest = remote(
        MASK_TWO, mask.at[pl.ds(ahead, rows - ahead), :, other],
        mbuf.at[pl.ds(par * rows + ahead, rows - ahead)], mate,
    )

    def zero_y(buf):
        zero = jnp.zeros((rows, RADIUS, depth), jnp.float32)

        @pl.when(jnp.logical_not(has_yl))
        def _():
            buf[:, 0:RADIUS, :] = zero

        @pl.when(jnp.logical_not(has_yr))
        def _():
            buf[:, RADIUS + ry :, :] = zero

    def zero_x(buf):
        zero = jnp.zeros((RADIUS, ry, half), jnp.float32)

        @pl.when(jnp.logical_not(has_xl))
        def _():
            buf[0:RADIUS] = zero

        @pl.when(jnp.logical_not(has_xr))
        def _():
            buf[RADIUS + 2 * rows :] = zero

    for buf in (dbuf, vback, oback):
        zero_y(buf)
    for buf in (abuf, vbuf, obuf):
        zero_x(buf)

    group = 4 if rows % 4 == 0 else 1
    l_des.wait()
    finish(r_des, has_yl, has_yr)
    filter_zy(dbuf, afull, group)
    r_a = remote(AFLD, afull.at[:, :, other], abuf.at[pl.ds(RADIUS + par * rows, rows)], mate)
    r_a.start()
    r_rest.start()
    r_sens = remote(SENS, sens.at[:, :, other], sbuf.at[my_rows], mate)
    r_sens.start()
    l_a = pltpu.make_async_copy(afull.at[:, :, own], abuf.at[pl.ds(RADIUS + par * rows, rows)], local_sems.at[3])
    l_a.start()
    l_a.wait()
    r_a.wait_recv()
    x_a = x_pair(A_UP, A_DN, abuf)
    begin(x_a, has_xl, has_xr)
    l_mask.wait()
    r_mask.wait_recv()
    r_rest.wait_recv()
    finish(x_a, has_xl, has_xr)

    total_x, total_y = rows * nx, ry * ny
    wz = cover(par * half + lax.broadcasted_iota(jnp.int32, (8, half), 1), depth)

    phys_out[...] = jnp.zeros_like(phys_out)

    def stage_one(j, carry):
        tile = pl.ds(pl.multiple_of(j * 8, 8), 8)
        wy = cover(gy * ry + j * 8 + lax.broadcasted_iota(jnp.int32, (8, half), 0), total_y)
        wyz = wy * wz

        def emit(i, value):
            weight = wyz * cover(pair * (2 * rows) + i, total_x)
            inv = 1.0 / weight
            shifted = jnp.tanh(beta_value * (value * inv - eta_value))
            solid = mbuf[i, tile, :]
            free = (1 - solid).astype(jnp.float32)
            phys_out[...] += jnp.where(solid == 1, 1.0, (TANH_MID + shifted) * (1.0 / SCALE))
            vbuf[RADIUS + i, tile, :] = (beta_value / SCALE) * (1.0 - shifted * shifted) * free * inv

        filter_x(abuf, tile, emit)
        return carry

    lax.fori_loop(0, ry // 8, stage_one, 0)
    x_v = x_pair(V_UP, V_DN, vbuf)
    begin(x_v, has_xl, has_xr)
    finish(x_v, has_xl, has_xr)

    def x_only(src, dst):
        def body(j, carry):
            tile = pl.ds(pl.multiple_of(j * 8, 8), 8)

            def emit(i, value):
                dst[i, tile, :] = value

            filter_x(src, tile, emit)
            return carry

        lax.fori_loop(0, ry // 8, body, 0)

    x_only(vbuf, vx)
    r_vb = remote(VB, vx.at[mate_rows], vback.at[:, mid, own], mate)
    r_vb.start()
    l_vb = pltpu.make_async_copy(vx.at[my_rows], vback.at[:, mid, own], local_sems.at[4])
    l_vb.start()

    l_sens.wait()
    r_sens.wait_recv()

    def times(i, carry):
        obuf[RADIUS + i] = -sbuf[i] * vbuf[RADIUS + i]
        return carry

    lax.fori_loop(0, 2 * rows, times, 0)
    x_o = x_pair(O_UP, O_DN, obuf)
    begin(x_o, has_xl, has_xr)
    finish(x_o, has_xl, has_xr)
    x_only(obuf, ox)
    chunks = CHUNKS if rows % CHUNKS == 0 else 1
    step = rows // chunks
    r_ob = [
        remote(OB + c, ox.at[pl.ds((1 - par) * rows + c * step, step)],
               oback.at[pl.ds(c * step, step), mid, own], mate)
        for c in range(chunks)
    ]
    for one in r_ob:
        one.start()
    l_ob = pltpu.make_async_copy(ox.at[my_rows], oback.at[:, mid, own], local_sems.at[5])
    l_ob.start()

    l_vb.wait()
    r_vb.wait_recv()
    y_v = y_pair(VY_UP, VY_DN, vback, RADIUS, vback)
    begin(y_v, has_yl, has_yr)
    finish(y_v, has_yl, has_yr)
    filter_zy(vback, vol_out, group)

    l_full.wait()

    def along(turn, coord, size, place, box, send, recv):
        for k in range(1, size):
            peer = lax.rem(coord + k, size)
            pltpu.make_async_remote_copy(
                src_ref=box.at[turn, coord], dst_ref=box.at[turn, coord], send_sem=send.at[turn, k],
                recv_sem=recv.at[turn, coord], device_id=place(peer), device_id_type=MESH,
            ).start()
        for k in range(1, size):
            peer = lax.rem(coord + k, size)
            pltpu.make_async_remote_copy(
                src_ref=box.at[turn, peer], dst_ref=box.at[turn, peer], send_sem=send.at[turn, k],
                recv_sem=recv.at[turn, peer], device_id=place(peer), device_id_type=MESH,
            ).wait()
        out = box[turn, 0]
        for k in range(1, size):
            out = out + box[turn, k]
        return out

    def all_sum(turn, tile):
        ybox[turn, gy] = tile
        tile = along(turn, gy, ny, lambda peer: (gx, peer), ybox, y_send, y_recv)
        xbox[turn, gx] = tile
        tile = along(turn, gx, nx, lambda peer: (peer, gy), xbox, x_send, x_recv)
        return jnp.sum(tile, axis=1, keepdims=True)

    part = 32 if ry % 32 == 0 else 8
    pieces = ry // part

    def fold(x):
        out = x[0:8]
        for k in range(1, part // 8):
            out = out + x[8 * k : 8 * (k + 1)]
        res = out[:, 0:128]
        for k in range(1, depth // 128):
            res = res + out[:, 128 * k : 128 * (k + 1)]
        return res

    def leave(src, dst, sems, c):
        some = pl.ds(c * step, step)
        return pltpu.make_async_copy(src.at[some], dst.at[some], sems.at[c])

    def where_is(i):
        row = i // pieces
        start = pl.multiple_of(lax.rem(i, pieces) * part, 8)
        return row, pl.ds(start, part), pl.ds(RADIUS + start, part)

    def shift_of(lam, grad, swing, cell):
        up = jnp.maximum(grad, 0.0)
        down = jnp.maximum(-grad, 0.0)
        a_two = (0.25 * 1.001) * up + (0.25 * 0.001) * down + 0.25e-05 + lam * ((0.25 * 1.001) * swing)
        b_two = (0.25 * 0.001) * up + (0.25 * 1.001) * down + 0.25e-05 + lam * ((0.25 * 0.001) * swing)
        a_inv, b_inv = lax.rsqrt(a_two), lax.rsqrt(b_two)
        a_root, b_root = a_two * a_inv, b_two * b_inv
        inv = pl.reciprocal(a_root + b_root)
        raw = (0.5 * (b_root - a_root)) * inv
        low = jnp.maximum(-cell, -move_limit)
        high = jnp.minimum(1.0 - cell, move_limit)
        return a_root, b_root, a_inv, b_inv, inv, raw, low, high

    def dual_pass(lam, first, begin_at, number, start):
        def body(i, carry):
            row, ys, ds = where_is(i)
            swing = vol_out[row, ys, :]
            if first:
                swing = swing * (1 - full_mask[row, ys, :]).astype(jnp.float32)
                vol_out[row, ys, :] = swing
            a_root, b_root, a_inv, b_inv, inv, raw, low, high = shift_of(
                lam, obj_out[row, ys, :], swing, dbuf[row, ds, :]
            )
            point = jnp.clip(raw, low, high)
            p_one, q_one = (0.25 * 1.001) * swing, (0.25 * 0.001) * swing
            both = pl.reciprocal(asym_gap * asym_gap - point * point)
            r_up, r_low = (asym_gap + point) * both, (asym_gap - point) * both
            value_p, value_q = p_one * r_up, q_one * r_low
            moved = 0.5 * (a_root * b_inv * q_one - b_root * a_inv * p_one) * (inv * inv)
            change = jnp.where(
                jnp.logical_and(raw > low, raw < high), (value_p * r_up - value_q * r_low) * moved, 0.0
            )
            out = (carry[0] + fold(value_p + value_q), carry[1] + fold(change))
            if first:
                out = out + (carry[2] + fold(swing),)
            return out

        return lax.fori_loop(begin_at * pieces, (begin_at + number) * pieces, body, start)

    cells = float(rows * ry * depth)
    cell_count = cells * nx * ny
    index = lax.broadcasted_iota(jnp.int32, (8, 128), 0)

    def pack(parts):
        out = jnp.zeros((8, 128), jnp.float32)
        for k, one in enumerate(parts):
            out = jnp.where(index == k, jnp.sum(one, axis=0, keepdims=True), out)
        return out

    lam = jnp.full((1, 1), 1.0, jnp.float32)
    offset = None
    zero = jnp.zeros((8, 128), jnp.float32)

    l_ob.wait()
    y_o = []
    parts = (zero,) * 3
    for c in range(chunks + 1):
        if c < chunks:
            r_ob[c].wait_recv()
            piece = oback.at[pl.ds(c * step, step)]
            y_o.append(y_pair(OY_UP + c, OY_DN + c, piece, RADIUS, piece))
            begin(y_o[c], has_yl, has_yr)
        if c >= 1:
            finish(y_o[c - 1], has_yl, has_yr)
            filter_zy(oback, obj_out, step, (c - 1) * step, step)
            leave(obj_out, obj_hbm, obj_sems, c - 1).start()
            parts = dual_pass(lam, True, (c - 1) * step, step, parts)

    for turn in range(DUAL_ITERS):
        if turn > 0:
            parts = dual_pass(lam, False, 0, rows, (zero,) * 2)
        if turn == 0:
            phys = phys_out[:, 0:128]
            for k in range(1, half // 128):
                phys = phys + phys_out[:, 128 * k : 128 * (k + 1)]
            base = parts[2] * (0.25 * (1.001 + 0.001) / asym_gap)
            parts = (parts[0], parts[1], phys - base - volume_share * cells / 1024.0)
        sums = all_sum(turn, pack(parts))
        if turn == 0:
            offset = sums[2:3] / cell_count
        level = sums[0:1] / cell_count + offset
        rate = sums[1:2] / cell_count
        lam = lam * jnp.exp(-level / (lam * rate - 1e-06))

    def last(i, carry):
        row, ys, ds = where_is(i)
        cell = dbuf[row, ds, :]
        raw, low, high = shift_of(lam, obj_out[row, ys, :], vol_out[row, ys, :], cell)[5:]
        point = cell + jnp.clip(raw, low, high)
        new_out[row, ys, :] = jnp.where(full_mask[row, ys, :] == 1, cell, point)
        return carry

    for c in range(chunks):
        lax.fori_loop(c * step * pieces, (c + 1) * step * pieces, last, 0)
        leave(new_out, new_hbm, new_sems, c).start()
    lam_out[0, 0] = lam[0, 0]
    for c in range(chunks):
        leave(obj_out, obj_hbm, obj_sems, c).wait()
        leave(new_out, new_hbm, new_sems, c).wait()

    for one in (r_mask, r_rest, r_a, r_sens, r_vb, *r_ob):
        one.wait_send()
    for two in (r_des, y_v, *y_o):
        sent(two, has_yl, has_yr)
    for two in (x_a, x_v, x_o):
        sent(two, has_xl, has_xr)


def per_device(design, sensitivity, solid_mask):
    rows, ry, depth = design.shape
    half = depth // 2
    nx, ny = lax.axis_size("gx"), lax.axis_size("gy")
    f32 = jnp.float32
    block = (rows, ry, depth)
    wide = (rows, ry + 2 * RADIUS, depth)
    tall = (2 * rows + 2 * RADIUS, ry, half)
    strip = (2 * rows, ry, half)
    anywhere = pl.BlockSpec(memory_space=pl.ANY)
    dma = pltpu.SemaphoreType.DMA
    new_design, objective_grad, lam = pl.pallas_call(
        kernel,
        out_shape=(
            jax.ShapeDtypeStruct(block, f32),
            jax.ShapeDtypeStruct(block, f32),
            jax.ShapeDtypeStruct((1, 1), f32),
        ),
        in_specs=[anywhere] * 3,
        out_specs=(anywhere, anywhere, pl.BlockSpec(memory_space=pltpu.SMEM)),
        scratch_shapes=[
            pltpu.VMEM(block, f32),
            pltpu.VMEM(block, f32),
            pltpu.VMEM(block, f32),
            pltpu.VMEM((8, half), f32),
            pltpu.VMEM(block, jnp.int32),
            pltpu.VMEM(wide, f32),
            pltpu.VMEM(block, f32),
            pltpu.VMEM(tall, f32),
            pltpu.VMEM(strip, jnp.int32),
            pltpu.VMEM(strip, f32),
            pltpu.VMEM(tall, f32),
            pltpu.VMEM(tall, f32),
            pltpu.VMEM(strip, f32),
            pltpu.VMEM(strip, f32),
            pltpu.VMEM(wide, f32),
            pltpu.VMEM(wide, f32),
            pltpu.VMEM((DUAL_ITERS, ny, 8, 128), f32),
            pltpu.VMEM((DUAL_ITERS, nx, 8, 128), f32),
            dma((COUNT,)),
            dma((COUNT,)),
            dma((7,)),
            dma((DUAL_ITERS, ny)),
            dma((DUAL_ITERS, ny)),
            dma((DUAL_ITERS, nx)),
            dma((DUAL_ITERS, nx)),
            dma((CHUNKS,)),
            dma((CHUNKS,)),
        ],
        compiler_params=pltpu.CompilerParams(
            collective_id=0, has_side_effects=True, vmem_limit_bytes=56 * 1024 * 1024
        ),
    )(design, sensitivity, solid_mask)
    return new_design, objective_grad, lam.reshape(())


def solution(mesh):
    return jax.shard_map(
        per_device,
        mesh=mesh,
        in_specs=(P("gx", "gy", None), P("gx", "gy", None), P("gx", "gy", None)),
        out_specs=(P("gx", "gy", None), P("gx", "gy", None), P()),
        check_vma=False,
    )
```

profile of v0, /device:TPU:0, one launch (start us, length us, event | category | flops | bytes accessed | tf_op | source)
XLA Modules:
  0.0 155.2 jit_solution(12573402282634387265)
XLA Ops:
  0.6 148.1 %shard_map.58 = (f32[16,64,512]{2,1,0:T(8,128)}, f32[16,64,512]{2,1,0:T(8,128)}, f32[1,1]{1,0:T(1,128)}) custom-call(f32[16,64,512]{2,1,0:T(8,128)} %design.1, f32[16,64,512]{2,1,0:T(8,128)} %sens.1, s32[16,64,512]{2,1,0:T(8,128)} %mask.1), custom_call_target="tpu_custom_call" | custom-call | tf_op jit(solution)/shard_map/pallas_call | solution.py:473
  148.7 0.0 copy-start
  148.7 3.3 %copy.9 = f32[16,64,512]{2,1,0:T(8,128)} copy(f32[16,64,512]{2,1,0:T(8,128)} %get-tuple-element.12) | data formatting | bytes 4194304
  152.0 0.0 copy-done
  152.0 1.3 copy.10
Async XLA Ops:
  148.7 3.3 %copy-start = (f32[16,64,512]{2,1,0:T(8,128)S(1)}, f32[16,64,512]{2,1,0:T(8,128)}, u32[]{:S(2)}) copy-start(f32[16,64,512]{2,1,0:T(8,128)} %get-tuple-element.13) | copy-start | bytes 6291460
where the time goes:
time: 155 us
  Pallas kernels  148 us (95%)
  local copies, waits for them, and re-layouts  4.61 us (3%)
  between operations  2.47 us (2%)
    pallas_call x1, Pallas kernels, per_device(): pl.pallas_call(kernel, out_shape=(jax.ShapeDtypeStruct(block, f32), jax.S...  148 us
    unnamed x4, local copies, waits for them, and re-layouts  4.61 us

commit v1 on v0

v1 whole, which is shorter than its diff:
```python
import functools
import math

import jax
import jax.numpy as jnp
from jax import lax
from jax.experimental import pallas as pl
from jax.experimental.pallas import tpu as pltpu
from jax.sharding import PartitionSpec as P

RADIUS = 8
DUAL_ITERS = 2
SPAN = RADIUS + 1
MESH = pl.DeviceIdType.MESH

beta_value = 4.0
eta_value = 0.5
volume_share = 0.4
move_limit = 0.2
asym_gap = 0.5
TANH_MID = math.tanh(beta_value * eta_value)
SCALE = math.tanh(beta_value * eta_value) + math.tanh(beta_value * (1.0 - eta_value))


def missing(distance):
    out = jnp.maximum(RADIUS - distance, 0)
    return (out * (out + 1)) // 2


def cover(cell, total):
    return (SPAN * SPAN - missing(cell) - missing(total - 1 - cell)).astype(jnp.float32)


def split2(x):
    hi = x.astype(jnp.bfloat16)
    lo = (x - hi.astype(jnp.float32)).astype(jnp.bfloat16)
    return hi, lo


def filter_x(src, tile, emit):
    count = src.shape[0] - 2 * RADIUS
    load = lambda i: src[i, tile, :]
    box = load(0)
    for k in range(1, SPAN):
        box = box + load(k)
    window = [box]
    for n in range(1, SPAN):
        box = box + (load(n + RADIUS) - load(n - 1))
        window.append(box)
    total = window[0]
    for k in range(1, SPAN):
        total = total + window[k]
    emit(0, total)
    for i in range(1, count):
        n = i + RADIUS
        box = box + (load(n + RADIUS) - load(n - 1))
        total = total + (box - window[i - 1])
        window.append(box)
        emit(i, total)


def triangle(near, far):
    return jnp.maximum(SPAN - jnp.abs(near - far), 0).astype(jnp.float32).astype(jnp.bfloat16)


def filter_y(src, dst, first, group):
    total, wide, depth = src.shape
    ry = wide - 2 * RADIUS
    jj = lax.broadcasted_iota(jnp.int32, (ry, wide), 0)
    bb = lax.broadcasted_iota(jnp.int32, (ry, wide), 1)
    band = triangle(jj + RADIUS, bb)
    band = jnp.concatenate([band, band], 1)

    def body(g, carry):
        for r in range(group):
            row = g * group + r
            both = jnp.concatenate(split2(src[row]), 0)
            dst[first + row] = jnp.dot(band, both, preferred_element_type=jnp.float32)
        return carry

    lax.fori_loop(0, total // group, body, 0)


def gather_edge(src, first, total, lanes, turn, out):
    tiles = src.shape[1] // 8
    per = GROUPS // tiles
    lane = lax.broadcasted_iota(jnp.int32, (8, 128), 1) // 8

    def body(g, carry):
        packed = jnp.zeros((8, 128), jnp.float32)
        for i in range(GROUPS):
            one = src[first + g * per + i // tiles, pl.ds((i % tiles) * 8, 8), lanes]
            if i > 0:
                one = pltpu.roll(one, 8 * i, 1)
            packed = jnp.where(lane == lax.rem(i + turn, GROUPS), one, packed)
        out[g] = packed
        return carry

    lax.fori_loop(0, total // per, body, 0)


def filter_z(buf, first, total, edge, own_start, edge_start, group, post):
    _, ry, half = buf.shape
    tiles = ry // 8
    per = GROUPS // tiles
    kk = own_start + lax.broadcasted_iota(jnp.int32, (half, half), 1)
    cc = own_start + lax.broadcasted_iota(jnp.int32, (half, half), 0)
    band = triangle(cc, kk)
    kk = own_start + lax.broadcasted_iota(jnp.int32, (128, half), 1)
    cc = edge_start + lax.broadcasted_iota(jnp.int32, (128, half), 0)
    cross = triangle(cc, kk)
    weights = jnp.concatenate([band, band, cross, cross], 0)

    def body(g, carry):
        parts = []
        for r in range(group):
            row = g * group + r
            hi, lo = split2(buf[first + row])
            packed = edge[g * (group // per) + r // per]
            cols = []
            for t in range(tiles):
                i = (r % per) * tiles + t
                cols.append(packed if i == 0 else pltpu.roll(packed, 128 - 8 * i, 1))
            ehi, elo = split2(jnp.concatenate(cols, 0))
            parts.append(jnp.concatenate([hi, lo, ehi, elo], 1))
        out = jnp.dot(jnp.concatenate(parts, 0), weights, preferred_element_type=jnp.float32)
        for r in range(group):
            row = g * group + r
            buf[first + row] = post(row, out[r * ry : (r + 1) * ry])
        return carry

    lax.fori_loop(0, total // group, body, 0)


GROUPS = 16
CHUNKS = 4


def kernel(design, sens, mask, new_hbm, obj_hbm, lam_out, dwide, mbuf, sbuf, atall, vtall, otall, vwide, owide, vfull,
           ofull, vback, oback, dother, mother, new_own, new_other, phys_out, edge_out, edge_in, mbox, xbox, ybox,
           bulk_send, bulk_recv, mask_send, mask_recv, sens_send, sens_recv, x_send, x_recv, back_send, back_recv,
           local_sems, out_sems, m_send, m_recv, gx_send, gx_recv, gy_send, gy_recv):
    rows, ry, depth = design.shape
    half = depth // 2
    both = 2 * rows
    tiles = ry // 8
    gx, gy = lax.axis_index("gx"), lax.axis_index("gy")
    nx, ny = lax.axis_size("gx"), lax.axis_size("gy")
    par = lax.rem(gx, 2)
    pair = gx // 2
    partner = gx + 1 - 2 * par
    has_xl, has_xr = gx >= 2, gx < nx - 2
    has_yl, has_yr = gy >= 1, gy < ny - 1
    xl, xr, yl, yr = (gx - 2, gy), (gx + 2, gy), (gx, gy - 1), (gx, gy + 1)
    mate = (partner, gy)

    barrier = pltpu.get_barrier_semaphore()

    def greet(dev):
        pl.semaphore_signal(barrier, inc=1, device_id=dev, device_id_type=MESH)

    for k in range(1, nx):
        greet((lax.rem(gx + k, nx), gy))
    for k in range(1, ny):
        greet((gx, lax.rem(gy + k, ny)))

    own = pl.ds(pl.multiple_of(par * half, 128), half)
    other = pl.ds(pl.multiple_of((1 - par) * half, 128), half)
    my_rows = pl.ds(par * rows, rows)
    mate_rows = pl.ds((1 - par) * rows, rows)
    mid = pl.ds(RADIUS, ry)
    edge_lanes = pl.ds(pl.multiple_of((1 - par) * (half - 128), 128), 128)
    edge_turn = (1 - par) * (GROUPS - 1)
    edge_start = (1 - par) * half + par * (half - 128)

    def local(k, src, dst):
        return pltpu.make_async_copy(src, dst, local_sems.at[k])

    l_des = local(0, design.at[:, :, own], dwide.at[my_rows, mid, :])
    l_mask = local(1, mask.at[:, :, own], mbuf.at[my_rows])
    l_sens = local(2, sens.at[:, :, own], sbuf.at[my_rows])
    l_dother = local(3, design.at[:, :, other], dother)
    l_mother = local(4, mask.at[:, :, other], mother)
    for one in (l_des, l_mask, l_sens, l_dother, l_mother):
        one.start()
    pl.semaphore_wait(barrier, nx + ny - 2)

    def remote(src, dst, send, recv, dev):
        return pltpu.make_async_remote_copy(
            src_ref=src, dst_ref=dst, send_sem=send, recv_sem=recv, device_id=dev, device_id_type=MESH
        )

    def bulk(k, src, dst, dev):
        return remote(src, dst, bulk_send.at[k], bulk_recv.at[k], dev)

    def begin(two, low, high):
        pl.when(high)(lambda: two[0].start())
        pl.when(low)(lambda: two[1].start())

    def finish(two, low, high):
        pl.when(low)(lambda: two[0].wait_recv())
        pl.when(high)(lambda: two[1].wait_recv())

    def sent(two, low, high):
        pl.when(high)(lambda: two[0].wait_send())
        pl.when(low)(lambda: two[1].wait_send())

    def tile_of(j):
        return pl.ds(pl.multiple_of(lax.rem(j + tiles - 1, tiles) * 8, 8), 8)

    def mask_tile(j):
        tile = tile_of(j)
        return remote(mask.at[:, tile, other], mbuf.at[my_rows, tile, :], mask_send.at[j], mask_recv.at[j], mate)

    def sens_tile(j):
        tile = tile_of(j)
        return remote(sens.at[:, tile, other], sbuf.at[my_rows, tile, :], sens_send.at[j], sens_recv.at[j], mate)

    def start_all(make, first, last):
        def body(j, carry):
            make(j).start()
            return carry

        lax.fori_loop(first, last, body, 0)

    def x_pair(k, buf, j):
        tile = tile_of(j)
        up, dn = (2 * k) * tiles + j, (2 * k + 1) * tiles + j
        return (
            remote(buf.at[pl.ds(both, RADIUS), tile, :], buf.at[pl.ds(0, RADIUS), tile, :],
                   x_send.at[up], x_recv.at[up], xr),
            remote(buf.at[pl.ds(RADIUS, RADIUS), tile, :], buf.at[pl.ds(RADIUS + both, RADIUS), tile, :],
                   x_send.at[dn], x_recv.at[dn], xl),
        )

    def y_pair(k, buf, some):
        return (
            bulk(k, buf.at[some, pl.ds(ry, RADIUS), :], buf.at[some, pl.ds(0, RADIUS), :], yr),
            bulk(k + 1, buf.at[some, pl.ds(RADIUS, RADIUS), :], buf.at[some, pl.ds(RADIUS + ry, RADIUS), :], yl),
        )

    every = pl.ds(0, both)
    r_des = bulk(0, design.at[:, :, other], dwide.at[my_rows, mid, :], mate)
    r_des.start()
    y_own = (
        bulk(1, design.at[:, pl.ds(ry - RADIUS, RADIUS), own], dwide.at[my_rows, pl.ds(0, RADIUS), :], yr),
        bulk(2, design.at[:, pl.ds(0, RADIUS), own], dwide.at[my_rows, pl.ds(RADIUS + ry, RADIUS), :], yl),
    )
    begin(y_own, has_yl, has_yr)
    start_all(mask_tile, 0, EARLY_MASK)

    def zero_y(buf):
        zero = jnp.zeros((both, RADIUS, half), jnp.float32)

        @pl.when(jnp.logical_not(has_yl))
        def _():
            buf[:, 0:RADIUS, :] = zero

        @pl.when(jnp.logical_not(has_yr))
        def _():
            buf[:, RADIUS + ry :, :] = zero

    def zero_x(buf):
        zero = jnp.zeros((RADIUS, ry, half), jnp.float32)

        @pl.when(jnp.logical_not(has_xl))
        def _():
            buf[0:RADIUS] = zero

        @pl.when(jnp.logical_not(has_xr))
        def _():
            buf[RADIUS + both :] = zero

    for buf in (dwide, vwide, owide):
        zero_y(buf)
    for buf in (atall, vtall, otall):
        zero_x(buf)
    phys_out[...] = jnp.zeros_like(phys_out)

    def edge_copy(k):
        return bulk(9 + k, edge_out.at[k], edge_in.at[k], mate)

    def send_edge(k, buf, first):
        gather_edge(buf, first, both, edge_lanes, edge_turn, edge_out.at[k])
        edge_copy(k).start()

    def finish_z(k, buf, first, post):
        edge_copy(k).wait_recv()
        filter_z(buf, first, both, edge_in.at[k], par * half, edge_start, 4, post)

    l_des.wait()
    r_des.wait_recv()
    y_mate = y_pair(3, dwide, mate_rows)
    begin(y_mate, has_yl, has_yr)
    finish(y_own, has_yl, has_yr)
    finish(y_mate, has_yl, has_yr)
    filter_y(dwide, atall, RADIUS, 2)
    send_edge(0, atall, RADIUS)
    start_all(mask_tile, EARLY_MASK, tiles)
    start_all(sens_tile, 0, EARLY_SENS)
    finish_z(0, atall, RADIUS, lambda row, out: out)

    def start_x(k, buf):
        def body(j, carry):
            begin(x_pair(k, buf, j), has_xl, has_xr)
            return carry

        lax.fori_loop(0, tiles, body, 0)

    start_x(0, atall)
    l_mask.wait()
    total_x, total_y = rows * nx, ry * ny
    wz = cover(par * half + lax.broadcasted_iota(jnp.int32, (8, half), 1), depth)

    def stage_one(j, carry):
        tile = tile_of(j)
        start = lax.rem(j + tiles - 1, tiles) * 8
        wy = cover(gy * ry + start + lax.broadcasted_iota(jnp.int32, (8, half), 0), total_y)
        wyz = wy * wz
        finish(x_pair(0, atall, j), has_xl, has_xr)
        mask_tile(j).wait_recv()

        def emit(i, value):
            weight = wyz * cover(pair * both + i, total_x)
            inv = 1.0 / weight
            shifted = jnp.tanh(beta_value * (value * inv - eta_value))
            solid = mbuf[i, tile, :]
            free = (1 - solid).astype(jnp.float32)
            phys_out[...] += jnp.where(solid == 1, 1.0, (TANH_MID + shifted) * (1.0 / SCALE))
            vtall[RADIUS + i, tile, :] = (beta_value / SCALE) * (1.0 - shifted * shifted) * free * inv

        filter_x(atall, tile, emit)
        begin(x_pair(1, vtall, j), has_xl, has_xr)
        return carry

    lax.fori_loop(0, tiles, stage_one, 0)

    def x_only(k, src, dst, y_two):
        def body(j, carry):
            tile = tile_of(j)
            into = pl.ds(pl.multiple_of(lax.rem(j + tiles - 1, tiles) * 8 + RADIUS, 8), 8)
            finish(x_pair(k, src, j), has_xl, has_xr)

            def emit(i, value):
                dst[i, into, :] = value

            filter_x(src, tile, emit)
            pl.when(jnp.logical_and(j == 0, has_yr))(lambda: y_two[0].start())
            pl.when(jnp.logical_and(j == 1, has_yl))(lambda: y_two[1].start())
            return carry

        lax.fori_loop(0, tiles, body, 0)

    y_v = y_pair(5, vwide, every)
    x_only(1, vtall, vwide, y_v)
    finish(y_v, has_yl, has_yr)
    filter_y(vwide, vfull, 0, 2)
    send_edge(1, vfull, 0)
    start_all(sens_tile, EARLY_SENS, tiles)
    l_sens.wait()

    def make_o(j, carry):
        tile = tile_of(j)
        sens_tile(j).wait_recv()

        def times(i, inner):
            for r in range(4):
                otall[RADIUS + 4 * i + r, tile, :] = -sbuf[4 * i + r, tile, :] * vtall[RADIUS + 4 * i + r, tile, :]
            return inner

        lax.fori_loop(0, both // 4, times, 0)
        begin(x_pair(2, otall, j), has_xl, has_xr)
        return carry

    lax.fori_loop(0, EARLY_SENS, make_o, 0)
    finish_z(1, vfull, 0, lambda row, out: out * (1 - mbuf[row]).astype(jnp.float32))

    def back(which, c):
        src, dst = ((vfull, vback), (ofull, oback))[which]
        k = which * rows + c
        return remote(src.at[(1 - par) * rows + c], dst.at[c], back_send.at[k], back_recv.at[k], mate)

    todo = [(which, c) for which in range(2) for c in range(rows)]

    def pump(number):
        for _ in range(min(number, len(todo))):
            which, c = todo.pop(0)
            back(which, c).start()

    pump(PUMP[0])
    lax.fori_loop(EARLY_SENS, tiles, make_o, 0)
    y_o = y_pair(7, owide, every)
    x_only(2, otall, owide, y_o)
    finish(y_o, has_yl, has_yr)
    filter_y(owide, ofull, 0, 2)
    send_edge(2, ofull, 0)
    pump(PUMP[1])
    finish_z(2, ofull, 0, lambda row, out: out)
    o_own = pltpu.make_async_copy(ofull.at[my_rows], obj_hbm.at[:, :, own], out_sems.at[0])
    o_own.start()
    pump(PUMP[2])

    def along(turn, coord, size, place, box, send, recv, after):
        for k in range(1, size):
            peer = lax.rem(coord + k, size)
            remote(box.at[turn, coord], box.at[turn, coord], send.at[turn, k], recv.at[turn, coord], place(peer)).start()
        after()
        for k in range(1, size):
            peer = lax.rem(coord + k, size)
            remote(box.at[turn, peer], box.at[turn, peer], send.at[turn, k], recv.at[turn, peer], place(peer)).wait()
        out = box[turn, 0]
        for k in range(1, size):
            out = out + box[turn, k]
        return out

    def all_sum(turn, tile, after):
        mbox[turn, par] = tile
        tile = along(turn, par, 2, lambda peer: (2 * pair + peer, gy), mbox, m_send, m_recv, after)
        xbox[turn, pair] = tile
        tile = along(turn, pair, nx // 2, lambda peer: (2 * peer + par, gy), xbox, gx_send, gx_recv, lambda: None)
        ybox[turn, gy] = tile
        tile = along(turn, gy, ny, lambda peer: (gx, peer), ybox, gy_send, gy_recv, lambda: None)
        return jnp.sum(tile, axis=1, keepdims=True)

    def fold(x):
        out = x[0:8]
        for k in range(1, x.shape[0] // 8):
            out = out + x[8 * k : 8 * (k + 1)]
        res = out[:, 0:128]
        for k in range(1, x.shape[1] // 128):
            res = res + out[:, 128 * k : 128 * (k + 1)]
        return res

    def shift_of(lam, grad, swing, cell):
        up = jnp.maximum(grad, 0.0)
        down = jnp.maximum(-grad, 0.0)
        a_two = (0.25 * 1.001) * up + (0.25 * 0.001) * down + 0.25e-05 + lam * ((0.25 * 1.001) * swing)
        b_two = (0.25 * 0.001) * up + (0.25 * 1.001) * down + 0.25e-05 + lam * ((0.25 * 0.001) * swing)
        a_inv, b_inv = lax.rsqrt(a_two), lax.rsqrt(b_two)
        a_root, b_root = a_two * a_inv, b_two * b_inv
        inv = pl.reciprocal(a_root + b_root)
        raw = (0.5 * (b_root - a_root)) * inv
        low = jnp.maximum(-cell, -move_limit)
        high = jnp.minimum(1.0 - cell, move_limit)
        return a_root, b_root, a_inv, b_inv, inv, raw, low, high

    part = 32 if ry % 32 == 0 else 8
    pieces = ry // part

    def dual_pass(lam, first, begin_at, end_at, start):
        def body(n, carry):
            i = n // pieces
            at = pl.multiple_of(lax.rem(n, pieces) * part, 8)
            ys, ds = pl.ds(at, part), pl.ds(RADIUS + at, part)
            swing = vfull[i, ys, :]
            a_root, b_root, a_inv, b_inv, inv, raw, low, high = shift_of(lam, ofull[i, ys, :], swing, dwide[i, ds, :])
            point = jnp.clip(raw, low, high)
            p_one, q_one = (0.25 * 1.001) * swing, (0.25 * 0.001) * swing
            recip = pl.reciprocal(asym_gap * asym_gap - point * point)
            r_up, r_low = (asym_gap + point) * recip, (asym_gap - point) * recip
            value_p, value_q = p_one * r_up, q_one * r_low
            moved = 0.5 * (a_root * b_inv * q_one - b_root * a_inv * p_one) * (inv * inv)
            change = jnp.where(
                jnp.logical_and(raw > low, raw < high), (value_p * r_up - value_q * r_low) * moved, 0.0
            )
            out = (carry[0] + fold(value_p + value_q), carry[1] + fold(change))
            if first:
                out = out + (carry[2] + fold(swing),)
            return out

        return lax.fori_loop(begin_at * pieces, end_at * pieces, body, start)

    cells = float(rows * ry * depth)
    cell_count = cells * nx * ny
    index = lax.broadcasted_iota(jnp.int32, (8, 128), 0)

    def pack(parts):
        out = jnp.zeros((8, 128), jnp.float32)
        for k, one in enumerate(parts):
            out = jnp.where(index == k, jnp.sum(one, axis=0, keepdims=True), out)
        return out

    lam = jnp.full((1, 1), 1.0, jnp.float32)
    offset = None
    zero = jnp.zeros((8, 128), jnp.float32)
    span = both // SEGMENTS
    for turn in range(DUAL_ITERS):
        parts = (zero,) * (3 if turn == 0 else 2)
        for seg in range(SEGMENTS):
            parts = dual_pass(lam, turn == 0, seg * span, (seg + 1) * span, parts)
            if seg < SEGMENTS - 1:
                pump(PUMP[3])
        if turn == 0:
            phys = phys_out[:, 0:128]
            for k in range(1, half // 128):
                phys = phys + phys_out[:, 128 * k : 128 * (k + 1)]
            base = parts[2] * (0.25 * (1.001 + 0.001) / asym_gap)
            parts = (parts[0], parts[1], phys - base - volume_share * cells / 1024.0)
        sums = all_sum(turn, pack(parts), lambda: pump(PUMP[4]))
        if turn == 0:
            offset = sums[2:3] / cell_count
        level = sums[0:1] / cell_count + offset
        rate = sums[1:2] / cell_count
        lam = lam * jnp.exp(-level / (lam * rate - 1e-06))
    pump(len(todo))
    lam_out[0, 0] = lam[0, 0]

    def settle(lam, grad, swing, cell, solid):
        raw, low, high = shift_of(lam, grad, swing, cell)[5:]
        return jnp.where(solid == 1, cell, cell + jnp.clip(raw, low, high))

    chunks = CHUNKS if rows % CHUNKS == 0 else 1
    step = rows // chunks

    def leave(k, src, dst, lanes, c):
        some = pl.ds(c * step, step)
        return pltpu.make_async_copy(src.at[some], dst.at[some, :, lanes], out_sems.at[1 + k * chunks + c])

    def last_own(i, carry):
        row = par * rows + i
        new_own[i] = settle(lam, ofull[row], vfull[row], dwide[row, mid, :], mbuf[row])
        return carry

    for c in range(chunks):
        lax.fori_loop(c * step, (c + 1) * step, last_own, 0)
        leave(0, new_own, new_hbm, own, c).start()

    def arrived(c, carry):
        back(0, c).wait_recv()
        return carry

    lax.fori_loop(0, rows, arrived, 0)
    l_dother.wait()
    l_mother.wait()

    def last_other(i, carry):
        back(1, i).wait_recv()
        new_other[i] = settle(lam, oback[i], vback[i], dother[i], mother[i])
        return carry

    for c in range(chunks):
        lax.fori_loop(c * step, (c + 1) * step, last_other, 0)
        leave(1, oback, obj_hbm, other, c).start()
        leave(2, new_other, new_hbm, other, c).start()

    r_des.wait_send()
    for k in range(3):
        edge_copy(k).wait_send()
    for two in (y_own, y_mate, y_v, y_o):
        sent(two, has_yl, has_yr)

    def tile_sent(j, carry):
        mask_tile(j).wait_send()
        sens_tile(j).wait_send()
        for k, buf in enumerate((atall, vtall, otall)):
            sent(x_pair(k, buf, j), has_xl, has_xr)
        return carry

    lax.fori_loop(0, tiles, tile_sent, 0)

    def piece_sent(c, carry):
        back(0, c).wait_send()
        back(1, c).wait_send()
        return carry

    lax.fori_loop(0, rows, piece_sent, 0)
    o_own.wait()
    for c in range(chunks):
        leave(0, new_own, new_hbm, own, c).wait()
        leave(1, oback, obj_hbm, other, c).wait()
        leave(2, new_other, new_hbm, other, c).wait()


EARLY_MASK = 2
EARLY_SENS = 4
SEGMENTS = 4
PUMP = (3, 2, 2, 1, 5)


def per_device(design, sensitivity, solid_mask):
    rows, ry, depth = design.shape
    half = depth // 2
    both = 2 * rows
    tiles = ry // 8
    nx, ny = lax.axis_size("gx"), lax.axis_size("gy")
    f32 = jnp.float32
    block = (rows, ry, depth)
    wide = (both, ry + 2 * RADIUS, half)
    tall = (both + 2 * RADIUS, ry, half)
    strip = (both, ry, half)
    side = (rows, ry, half)
    edges = (3, both * tiles // GROUPS, 8, 128)
    anywhere = pl.BlockSpec(memory_space=pl.ANY)
    dma = pltpu.SemaphoreType.DMA
    vmem = pltpu.VMEM
    new_design, objective_grad, lam = pl.pallas_call(
        kernel,
        out_shape=(
            jax.ShapeDtypeStruct(block, f32),
            jax.ShapeDtypeStruct(block, f32),
            jax.ShapeDtypeStruct((1, 1), f32),
        ),
        in_specs=[anywhere] * 3,
        out_specs=(anywhere, anywhere, pl.BlockSpec(memory_space=pltpu.SMEM)),
        scratch_shapes=[
            vmem(wide, f32),
            vmem(strip, jnp.int32),
            vmem(strip, f32),
            vmem(tall, f32),
            vmem(tall, f32),
            vmem(tall, f32),
            vmem(wide, f32),
            vmem(wide, f32),
            vmem(strip, f32),
            vmem(strip, f32),
            vmem(side, f32),
            vmem(side, f32),
            vmem(side, f32),
            vmem(side, jnp.int32),
            vmem(side, f32),
            vmem(side, f32),
            vmem((8, half), f32),
            vmem(edges, f32),
            vmem(edges, f32),
            vmem((DUAL_ITERS, 2, 8, 128), f32),
            vmem((DUAL_ITERS, nx // 2, 8, 128), f32),
            vmem((DUAL_ITERS, ny, 8, 128), f32),
            dma((12,)),
            dma((12,)),
            dma((tiles,)),
            dma((tiles,)),
            dma((tiles,)),
            dma((tiles,)),
            dma((6 * tiles,)),
            dma((6 * tiles,)),
            dma((2 * rows,)),
            dma((2 * rows,)),
            dma((5,)),
            dma((1 + 3 * CHUNKS,)),
            dma((DUAL_ITERS, 2)),
            dma((DUAL_ITERS, 2)),
            dma((DUAL_ITERS, nx // 2)),
            dma((DUAL_ITERS, nx // 2)),
            dma((DUAL_ITERS, ny)),
            dma((DUAL_ITERS, ny)),
        ],
        compiler_params=pltpu.CompilerParams(
            collective_id=0, has_side_effects=True, vmem_limit_bytes=56 * 1024 * 1024
        ),
    )(design, sensitivity, solid_mask)
    return new_design, objective_grad, lam.reshape(())


def solution(mesh):
    return jax.shard_map(
        per_device,
        mesh=mesh,
        in_specs=(P("gx", "gy", None), P("gx", "gy", None), P("gx", "gy", None)),
        out_specs=(P("gx", "gy", None), P("gx", "gy", None), P()),
        check_vma=False,
    )
```

time: 155 us -> 154 us (level)
  Pallas kernels: 148 us -> 146 us
    pallas_call x1, Pallas kernels: 148 us -> 146 us  [per_device(): pl.pallas_call(kernel, out_shape=(jax.ShapeDtypeStruct(block, f32), jax.S...]
where the time goes in v1:
time: 154 us; the launch traced here: 153 us
  Pallas kernels  146 us (95%)
  local copies, waits for them, and re-layouts  4.61 us (3%)
  between operations  2.47 us (2%)
    pallas_call x1, Pallas kernels, per_device(): pl.pallas_call(kernel, out_shape=(jax.ShapeDtypeStruct(block, f32), jax.S...  146 us
    unnamed x4, local copies, waits for them, and re-layouts  4.61 us

profile of v1, /device:TPU:0, one launch (start us, length us, event | category | flops | bytes accessed | tf_op | source)
XLA Modules:
  0.0 153.3 jit_solution(11167901295225121530)
XLA Ops:
  0.6 146.3 %shard_map.58 = (f32[16,64,512]{2,1,0:T(8,128)}, f32[16,64,512]{2,1,0:T(8,128)}, f32[1,1]{1,0:T(1,128)}) custom-call(f32[16,64,512]{2,1,0:T(8,128)} %design.1, f32[16,64,512]{2,1,0:T(8,128)} %sens.1, s32[16,64,512]{2,1,0:T(8,128)} %mask.1), custom_call_target="tpu_custom_call" | custom-call | tf_op jit(solution)/shard_map/pallas_call | solution.py:596
  146.9 0.0 copy-start
  146.9 3.3 %copy.9 = f32[16,64,512]{2,1,0:T(8,128)} copy(f32[16,64,512]{2,1,0:T(8,128)} %get-tuple-element.12) | data formatting | bytes 4194304
  150.2 0.0 copy-done
  150.2 1.3 copy.10
Async XLA Ops:
  146.9 3.3 %copy-start = (f32[16,64,512]{2,1,0:T(8,128)S(1)}, f32[16,64,512]{2,1,0:T(8,128)}, u32[]{:S(2)}) copy-start(f32[16,64,512]{2,1,0:T(8,128)} %get-tuple-element.13) | copy-start | bytes 6291460

commit v2 on v1

--- a/solution.py
+++ b/solution.py
@@ -286,7 +286,7 @@
 
     def finish_z(k, buf, first, post):
         edge_copy(k).wait_recv()
-        filter_z(buf, first, both, edge_in.at[k], par * half, edge_start, 4, post)
+        filter_z(buf, first, both, edge_in.at[k], par * half, edge_start, 8, post)
 
     l_des.wait()
     r_des.wait_recv()
@@ -294,7 +294,7 @@
     begin(y_mate, has_yl, has_yr)
     finish(y_own, has_yl, has_yr)
     finish(y_mate, has_yl, has_yr)
-    filter_y(dwide, atall, RADIUS, 2)
+    filter_y(dwide, atall, RADIUS, 8)
     send_edge(0, atall, RADIUS)
     start_all(mask_tile, EARLY_MASK, tiles)
     start_all(sens_tile, 0, EARLY_SENS)
@@ -335,26 +335,29 @@
 
     lax.fori_loop(0, tiles, stage_one, 0)
 
-    def x_only(k, src, dst, y_two):
+    def x_tile(k, src, dst, y_two, j):
+        tile = tile_of(j)
+        into = pl.ds(pl.multiple_of(lax.rem(j + tiles - 1, tiles) * 8 + RADIUS, 8), 8)
+        finish(x_pair(k, src, j), has_xl, has_xr)
+
+        def emit(i, value):
+            dst[i, into, :] = value
+
+        filter_x(src, tile, emit)
+        pl.when(jnp.logical_and(j == 0, has_yr))(lambda: y_two[0].start())
+        pl.when(jnp.logical_and(j == 1, has_yl))(lambda: y_two[1].start())
+
+    def x_only(k, src, dst, y_two, first):
         def body(j, carry):
-            tile = tile_of(j)
-            into = pl.ds(pl.multiple_of(lax.rem(j + tiles - 1, tiles) * 8 + RADIUS, 8), 8)
-            finish(x_pair(k, src, j), has_xl, has_xr)
-
-            def emit(i, value):
-                dst[i, into, :] = value
-
-            filter_x(src, tile, emit)
-            pl.when(jnp.logical_and(j == 0, has_yr))(lambda: y_two[0].start())
-            pl.when(jnp.logical_and(j == 1, has_yl))(lambda: y_two[1].start())
+            x_tile(k, src, dst, y_two, j)
             return carry
 
-        lax.fori_loop(0, tiles, body, 0)
+        lax.fori_loop(first, tiles, body, 0)
 
     y_v = y_pair(5, vwide, every)
-    x_only(1, vtall, vwide, y_v)
+    x_only(1, vtall, vwide, y_v, 0)
     finish(y_v, has_yl, has_yr)
-    filter_y(vwide, vfull, 0, 2)
+    filter_y(vwide, vfull, 0, 8)
     send_edge(1, vfull, 0)
     start_all(sens_tile, EARLY_SENS, tiles)
     l_sens.wait()
@@ -388,11 +391,17 @@
             back(which, c).start()
 
     pump(PUMP[0])
-    lax.fori_loop(EARLY_SENS, tiles, make_o, 0)
     y_o = y_pair(7, owide, every)
-    x_only(2, otall, owide, y_o)
+
+    def o_step(j, carry):
+        make_o(j, carry)
+        x_tile(2, otall, owide, y_o, j - EARLY_SENS)
+        return carry
+
+    lax.fori_loop(EARLY_SENS, tiles, o_step, 0)
+    x_only(2, otall, owide, y_o, tiles - EARLY_SENS)
     finish(y_o, has_yl, has_yr)
-    filter_y(owide, ofull, 0, 2)
+    filter_y(owide, ofull, 0, 8)
     send_edge(2, ofull, 0)
     pump(PUMP[1])
     finish_z(2, ofull, 0, lambda row, out: out)
@@ -574,7 +583,8 @@
 EARLY_MASK = 2
 EARLY_SENS = 4
 SEGMENTS = 4
-PUMP = (3, 2, 2, 1, 5)
+PUMP = (7, 4, 2, 1, 7)
+VMEM_MIB = 48
 
 
 def per_device(design, sensitivity, solid_mask):
@@ -600,7 +610,7 @@
             jax.ShapeDtypeStruct(block, f32),
             jax.ShapeDtypeStruct((1, 1), f32),
         ),
-        in_specs=[anywhere] * 3,
+        in_specs=[pl.BlockSpec(memory_space=pltpu.HBM)] * 3,
         out_specs=(anywhere, anywhere, pl.BlockSpec(memory_space=pltpu.SMEM)),
         scratch_shapes=[
             vmem(wide, f32),
@@ -645,7 +655,7 @@
             dma((DUAL_ITERS, ny)),
         ],
         compiler_params=pltpu.CompilerParams(
-            collective_id=0, has_side_effects=True, vmem_limit_bytes=56 * 1024 * 1024
+            collective_id=0, has_side_effects=True, vmem_limit_bytes=VMEM_MIB * 1024 * 1024
         ),
     )(design, sensitivity, solid_mask)
     return new_design, objective_grad, lam.reshape(())

time: 154 us -> 137 us (0.89)
  Pallas kernels: 146 us -> 132 us
  local copies, waits for them, and re-layouts: 4.61 us -> 2.64 us
    pallas_call x1, Pallas kernels: 146 us -> 132 us  [per_device(): pl.pallas_call(kernel, out_shape=(jax.ShapeDtypeStruct(block, f32), jax.S...]
    unnamed x4 -> x2, local copies, waits for them, and re-layouts: 4.61 us -> 2.64 us
where the time goes in v2:
time: 137 us
  Pallas kernels  132 us (96%)
  local copies, waits for them, and re-layouts  2.64 us (2%)
  between operations  2.33 us (2%)
    pallas_call x1, Pallas kernels, per_device(): pl.pallas_call(kernel, out_shape=(jax.ShapeDtypeStruct(block, f32), jax.S...  132 us

profile of v2, /device:TPU:0, one launch (start us, length us, event | category | flops | bytes accessed | tf_op | source)
XLA Modules:
  0.0 137.0 jit_solution(12735781438806138596)
XLA Ops:
  0.6 132.0 %shard_map.58 = (f32[16,64,512]{2,1,0:T(8,128)S(1)}, f32[16,64,512]{2,1,0:T(8,128)S(1)}, f32[1,1]{1,0:T(1,128)}) custom-call(f32[16,64,512]{2,1,0:T(8,128)} %design.1, f32[16,64,512]{2,1,0:T(8,128)} %sens.1, s32[16,64,512]{2,1,0:T(8,128)} %mask.1), custom_call_target="tpu_custom_call" | custom-call | tf_op jit(solution)/shard_map/pallas_call | solution.py:606
  132.6 1.3 copy.9
  133.9 1.3 copy.10

commit v3 on v2

--- a/solution.py
+++ b/solution.py
@@ -375,7 +375,15 @@
         begin(x_pair(2, otall, j), has_xl, has_xr)
         return carry
 
-    lax.fori_loop(0, EARLY_SENS, make_o, 0)
+    y_o = y_pair(7, owide, every)
+
+    def o_step(j, carry):
+        make_o(j, carry)
+        x_tile(2, otall, owide, y_o, j - LAG)
+        return carry
+
+    lax.fori_loop(0, LAG, make_o, 0)
+    lax.fori_loop(LAG, EARLY_SENS, o_step, 0)
     finish_z(1, vfull, 0, lambda row, out: out * (1 - mbuf[row]).astype(jnp.float32))
 
     def back(which, c):
@@ -391,15 +399,8 @@
             back(which, c).start()
 
     pump(PUMP[0])
-    y_o = y_pair(7, owide, every)
-
-    def o_step(j, carry):
-        make_o(j, carry)
-        x_tile(2, otall, owide, y_o, j - EARLY_SENS)
-        return carry
-
     lax.fori_loop(EARLY_SENS, tiles, o_step, 0)
-    x_only(2, otall, owide, y_o, tiles - EARLY_SENS)
+    x_only(2, otall, owide, y_o, tiles - LAG)
     finish(y_o, has_yl, has_yr)
     filter_y(owide, ofull, 0, 8)
     send_edge(2, ofull, 0)
@@ -580,10 +581,11 @@
         leave(2, new_other, new_hbm, other, c).wait()
 
 
-EARLY_MASK = 2
-EARLY_SENS = 4
+EARLY_MASK = 3
+EARLY_SENS = 6
+LAG = 3
 SEGMENTS = 4
-PUMP = (7, 4, 2, 1, 7)
+PUMP = (6, 4, 2, 1, 7)
 VMEM_MIB = 48
 
 

time: 137 us -> 133 us (0.971)
  Pallas kernels: 132 us -> 128 us
    pallas_call x1, Pallas kernels: 132 us -> 128 us  [per_device(): pl.pallas_call(kernel, out_shape=(jax.ShapeDtypeStruct(block, f32), jax.S...]
where the time goes in v3:
time: 133 us
  Pallas kernels  128 us (96%)
  local copies, waits for them, and re-layouts  2.64 us (2%)
  between operations  2.33 us (2%)
    pallas_call x1, Pallas kernels, per_device(): pl.pallas_call(kernel, out_shape=(jax.ShapeDtypeStruct(block, f32), jax.S...  128 us

profile of v3, /device:TPU:0, one launch (start us, length us, event | category | flops | bytes accessed | tf_op | source)
XLA Modules:
  0.0 133.1 jit_solution(702552063831959702)
XLA Ops:
  0.6 128.1 %shard_map.58 = (f32[16,64,512]{2,1,0:T(8,128)S(1)}, f32[16,64,512]{2,1,0:T(8,128)S(1)}, f32[1,1]{1,0:T(1,128)}) custom-call(f32[16,64,512]{2,1,0:T(8,128)} %design.1, f32[16,64,512]{2,1,0:T(8,128)} %sens.1, s32[16,64,512]{2,1,0:T(8,128)} %mask.1), custom_call_target="tpu_custom_call" | custom-call | tf_op jit(solution)/shard_map/pallas_call | solution.py:608
  128.7 1.3 copy.9
  130.1 1.3 copy.10
